TPU v7x, 32 devices: a whole 2x2x4 slice. The times are simulated.
32 devices in a mesh: dp: 16 (over z, y, core), rows: 2 (over x).
Axes of the slice: x: 2, y: 2, z: 4, core: 2. Of those that a mesh axis runs over, the one named last changes fastest.
Arguments:
- latents: bfloat16 [16, 4, 128, 320], P('dp', 'rows'), may hold values from -6 to 6
- mean_one: float32 [16, 32], P('dp'), may hold values from -0.5 to 0.5
- rstd_one: float32 [16, 32], P('dp'), may hold values from 0.5 to 2
- gain_one: float32 [320], replicated, may hold values from 0.25 to 1.75
- shift_one: float32 [320], replicated, may hold values from -0.5 to 0.5
- kernel_one: bfloat16 [4, 9, 25600], P(None, None, 'dp'), may hold values from -0.109375 to 0.109375
- bias_one: float32 [320], replicated, may hold values from -3 to 3
- embed_bias: float32 [16, 320], P('dp'), may hold values from -3 to 3
- mean_two: float32 [16, 32], P('dp'), may hold values from -0.5 to 0.5
- rstd_two: float32 [16, 32], P('dp'), may hold values from 0.5 to 2
- gain_two: float32 [320], replicated, may hold values from 0.25 to 1.75
- shift_two: float32 [320], replicated, may hold values from -0.5 to 0.5
- kernel_two: bfloat16 [4, 9, 25600], P(None, None, 'dp'), may hold values from -0.109375 to 0.109375
- bias_two: float32 [320], replicated, may hold values from -3 to 3
Outputs:
- block_out: bfloat16 [16, 4, 128, 320], P('dp', 'rows')
All inputs are finite; a program needn't handle non-finite values.
Results may differ from a plain program's by a relative error of at most 0.0045.
Values may be sent and summed in bfloat16 or wider, within the bound.
No kernel may reach another device: no remote copies, remote signals or barrier semaphores. Data moves between devices by JAX's collectives and lax.ppermute only.
A program may use at most 192 MiB of HBM per device.

v0:
```python
import jax
import jax.numpy as jnp
from jax import lax
from jax.sharding import PartitionSpec as P


def padded_2(array, sides, width):
    for axis, dim in sides:
        devices, length = (lax.axis_size(axis), array.shape[dim])
        up = [(i, (i + 1) % devices) for i in range(devices - 1)]
        down = [(j, i) for i, j in up]
        last = lax.slice_in_dim(array, length - width, length, axis=dim)
        first = lax.slice_in_dim(array, 0, width, axis=dim)
        before = lax.ppermute(last, axis, up)
        after = lax.ppermute(first, axis, down)
        array = jnp.concatenate([before, array, after], axis=dim)
    return array


def norm_silu(values, group_mean, group_rstd, gain_vec, shift_vec):
    height, columns, channels = values.shape
    groups = group_mean.shape[-1]
    grouped = values.reshape(height, columns, groups, channels // groups)
    scaled = (grouped - group_mean[0][:, None]) * group_rstd[0][:, None]
    return jax.nn.silu(scaled.reshape(height, columns, channels) * gain_vec + shift_vec)


def padded_rows(activation):
    padded = padded_2(activation, (("rows", 0),), 1)
    return jnp.pad(padded, ((0, 0), (1, 1), (0, 0)))


def window_at(padded, position, height, columns, first_channel, depth):
    tap_row = position // 3
    tap_col = position % 3
    window = padded[
        tap_row : tap_row + height,
        tap_col : tap_col + columns,
        first_channel : first_channel + depth,
    ]
    return window.reshape(height * columns, depth)


def reorder_whole(whole_kernel, channels):
    blocks = whole_kernel.shape[0]
    split = whole_kernel.reshape(blocks, 9, channels // blocks, channels)
    return jnp.transpose(split, (1, 0, 2, 3)).reshape(3, 3 * channels, channels)


def whole_weights(kernel, channels):
    whole_kernel = lax.all_gather(kernel, "dp", axis=2, tiled=True)
    return reorder_whole(whole_kernel, channels)


def convolve_whole(activation, weights):
    height, columns, channels = activation.shape
    padded = padded_rows(activation)
    accumulated = jnp.zeros((height * columns, channels), jnp.float32)
    for tap_row in range(3):
        windows = jnp.concatenate(
            [
                window_at(padded, 3 * tap_row + tap_col, height, columns, 0, channels)
                for tap_col in range(3)
            ],
            axis=1,
        )
        accumulated = accumulated + jnp.dot(
            windows, weights[tap_row], preferred_element_type=jnp.float32
        )
    return accumulated.reshape(height, columns, channels)


def shards(
    latents,
    mean_one,
    rstd_one,
    gain_one,
    shift_one,
    kernel_one,
    bias_one,
    embed_bias,
    mean_two,
    rstd_two,
    gain_two,
    shift_two,
    kernel_two,
    bias_two,
):
    channels = latents.shape[3]
    sample = latents[0].astype(jnp.float32)
    first_act = norm_silu(sample, mean_one, rstd_one, gain_one, shift_one).astype(jnp.bfloat16)
    hidden = (
        convolve_whole(first_act, whole_weights(kernel_one, channels)) + bias_one + embed_bias[0]
    )
    second_act = norm_silu(hidden, mean_two, rstd_two, gain_two, shift_two).astype(jnp.bfloat16)
    result = convolve_whole(second_act, whole_weights(kernel_two, channels)) + bias_two + sample
    return result.astype(jnp.bfloat16)[None]


def solution(mesh):
    placed = (
        P("dp", "rows", None, None),
        P("dp", None),
        P("dp", None),
        P(),
        P(),
        P(None, None, "dp"),
        P(),
        P("dp", None),
        P("dp", None),
        P("dp", None),
        P(),
        P(),
        P(None, None, "dp"),
        P(),
    )
    return jax.shard_map(
        shards, mesh=mesh, in_specs=placed, out_specs=P("dp", "rows", None, None), check_vma=False
    )
```

profile of v0, /device:TPU:0, one launch (start us, length us, event | category | flops | bytes accessed | tf_op | source)
XLA Modules:
  0.0 321.2 jit_solution(16401829512371649083)
XLA Ops:
  6.5 0.0 all-gather.3.cloned.1.call-start
  6.5 3.1 copy.65
  9.7 0.0 all-gather.3.cloned.1.call-update
  9.7 0.0 copy-start.11
  9.7 0.0 copy-start.12
  9.7 0.0 copy-start
  9.7 0.0 copy-start.4
  9.7 0.0 copy-start.5
  9.7 0.0 all-gather.5.cloned.1.call-start
  9.8 2.4 copy.77
  12.2 0.0 all-gather.5.cloned.1.call-update
  12.2 0.0 copy-start.10
  12.2 0.1 mul.80
  12.3 0.1 mul.81
  12.4 0.1 sub.41
  12.5 0.1 sub.42
  12.6 0.0 copy-done
  12.6 0.0 copy-done.4
  12.6 0.0 copy-done.5
  12.6 0.3 multiply_convert_fusion.3
  12.9 4.9 %collective-permute-start = (bf16[1,128,320]{1,2,0:T(8,128)(2,1)S(1)}, bf16[1,128,320]{1,2,0:T(8,128)(2,1)S(1)}, u32[]{:S(2)}, u32[]{:S(2)}) collective-permute-start(bf16[1,128,320]{1,2,0:T(8,128)(2,1)S(1)} %get-tuple-element.29), channel_id=1, source_target_pairs={{0,1},{2,3},{4,5},{6,7},{8,9},{10,11},{12,13},{14,15},{16,17},{18,... | collective-permute-start | bytes 245768 | tf_op jit(solution)/shard_map/ppermute | solution.py:14
  17.8 1.3 collective-permute-start.1
  19.1 0.2 copy.68
  19.3 0.9 multiply_convert_fusion.2
  20.2 0.0 copy-done.13
  20.2 0.1 mul.93
  20.3 0.1 mul.94
  20.4 0.1 sub.48
  20.4 0.1 sub.49
  20.6 0.0 collective-permute-done
  20.6 3.5 %collective-permute-done.1 = bf16[1,128,320]{1,2,0:T(8,128)(2,1)S(1)} collective-permute-done((bf16[1,128,320]{1,2,0:T(8,128)(2,1)S(1)}, bf16[1,128,320]{1,2,0:T(8,128)(2,1)S(1)}, u32[]{:S(2)}, u32[]{:S(2)}) %collective-permute-start.1) | collective-permute-done | bytes 81952 | tf_op jit(solution)/shard_map/ppermute | solution.py:15
  24.2 0.3 fusion.5
  24.5 0.2 slice_bitcast_fusion.7
  24.8 0.7 copy_bitcast_fusion.11
  25.5 120.5 %all-gather.3.cloned.1.call-done = bf16[4,9,25600]{1,0,2:T(4,128)(2,1)} async-done(((bf16[4,9,1600]{1,0,2:T(4,128)(2,1)}), bf16[4,9,25600]{1,0,2:T(4,128)(2,1)}) %all-gather.3.cloned.1.call-update) | async-done | bytes 1843216 | tf_op jit(solution)/shard_map/all_gather | solution.py:51
  146.0 30.0 %copy.66 = bf16[4,9,80,320]{3,2,0,1:T(8,128)(2,1)S(1)} copy(bf16[4,9,80,320]{1,0,3,2:T(4,128)(2,1)} %bitcast.136) | data formatting | bytes 3686400 | tf_op jit(solution)/shard_map/reshape | solution.py:46
  176.1 0.2 fusion.62
  176.3 0.0 copy-start.1
  176.3 0.0 copy-start.2
  176.3 0.4 fusion.6
  176.8 0.0 copy-start.6
  176.8 0.0 copy-start.7
  176.8 0.0 copy-start.8
  176.8 0.4 copy-done.1
  177.2 0.1 copy-done.2
  177.3 0.4 convolution_add_fusion.3
  177.8 0.6 multiply_convert_fusion
  178.4 0.3 multiply_convert_fusion.1
  178.8 3.4 %collective-permute-start.2 = (bf16[1,128,320]{1,2,0:T(8,128)(2,1)S(1)}, bf16[1,128,320]{1,2,0:T(8,128)(2,1)S(1)}, u32[]{:S(2)}, u32[]{:S(2)}) collective-permute-start(bf16[1,128,320]{1,2,0:T(8,128)(2,1)S(1)} %get-tuple-element.25), channel_id=1, source_target_pairs={{0,1},{2,3},{4,5},{6,7},{8,9},{10,11},{12,13},{14,15},{16,17},{18,... | collective-permute-start | bytes 245768 | tf_op jit(solution)/shard_map/ppermute | solution.py:14
  182.2 1.3 collective-permute-start.3
  183.5 97.6 %all-gather.5.cloned.1.call-done = bf16[4,9,25600]{1,0,2:T(4,128)(2,1)} async-done(((bf16[4,9,1600]{1,0,2:T(4,128)(2,1)}), bf16[4,9,25600]{1,0,2:T(4,128)(2,1)}) %all-gather.5.cloned.1.call-update) | async-done | bytes 1843216 | tf_op jit(solution)/shard_map/all_gather | solution.py:51
  281.1 29.7 %copy.78 = bf16[4,9,80,320]{3,2,0,1:T(8,128)(2,1)S(1)} copy(bf16[4,9,80,320]{1,0,3,2:T(4,128)(2,1)} %bitcast.135) | data formatting | bytes 3686400 | tf_op jit(solution)/shard_map/reshape | solution.py:46
  310.8 0.2 fusion.61
  311.1 0.0 collective-permute-done.2
  311.1 0.0 collective-permute-done.3
  311.2 0.3 select_maximum_fusion
  311.5 0.2 slice_bitcast_fusion.1
  312.0 0.4 fusion.22
  312.4 0.4 convolution_add_fusion.1
  312.9 0.0 copy-start.9
  312.9 0.4 convolution_add_fusion
  313.3 0.2 reshape.141
  313.5 0.1 copy-done.9
  313.5 0.8 fusion.50
  (27 shorter events, 0.5 us)
Async XLA Ops:
  6.5 3.3 %copy-start.3 = (bf16[4,9,1600]{2,0,1:T(4,128)(2,1)S(1)}, bf16[4,9,1600]{2,0,1:T(4,128)(2,1)}, u32[]{:S(2)}) copy-start(bf16[4,9,1600]{2,0,1:T(4,128)(2,1)} %param.26) | copy-start | bytes 345604
  6.5 139.5 %all-gather.3.cloned.1.call-start = ((), (), s32[]{:S(2)}) async-start(), calls=%async_computation | async-start | bytes 27852800 | tf_op jit(solution)/shard_map/all_gather | solution.py:51
  9.7 2.5 copy-start.11
  9.7 2.7 copy-start.12
  9.7 2.9 copy-start
  9.7 2.9 copy-start.4
  9.7 2.9 copy-start.5
  9.7 271.4 %all-gather.5.cloned.1.call-start = ((), (), s32[]{:S(2)}) async-start(), calls=%async_computation.1 | async-start | bytes 27852800 | tf_op jit(solution)/shard_map/all_gather | solution.py:51
  12.2 8.0 %copy-start.13 = (f32[1,32]{1,0:T(1,128)S(1)}, f32[1,32]{1,0:T(1,128)}, u32[]{:S(2)}) copy-start(f32[1,32]{1,0:T(1,128)} %param.23) | copy-start | bytes 388
  12.2 8.2 %copy-start.14 = (f32[1,32]{1,0:T(1,128)S(1)}, f32[1,32]{1,0:T(1,128)}, u32[]{:S(2)}) copy-start(f32[1,32]{1,0:T(1,128)} %param.22) | copy-start | bytes 388
  12.2 8.4 %copy-start.10 = (f32[1,320]{1,0:T(1,128)S(1)}, f32[1,320]{1,0:T(1,128)}, u32[]{:S(2)}) copy-start(f32[1,320]{1,0:T(1,128)} %param.21) | copy-start | bytes 3844
  12.9 7.7 %collective-permute-start = (bf16[1,128,320]{1,2,0:T(8,128)(2,1)S(1)}, bf16[1,128,320]{1,2,0:T(8,128)(2,1)S(1)}, u32[]{:S(2)}, u32[]{:S(2)}) collective-permute-start(bf16[1,128,320]{1,2,0:T(8,128)(2,1)S(1)} %get-tuple-element.29), channel_id=1, source_target_pairs={{0,1},{2,3},{4,5},{6,7},{8,9},{10,11},{12,13},{14,15},{16,17},{18,... | collective-permute-start | bytes 245768 | tf_op jit(solution)/shard_map/ppermute | solution.py:14
  17.8 6.3 %collective-permute-start.1 = (bf16[1,128,320]{1,2,0:T(8,128)(2,1)S(1)}, bf16[1,128,320]{1,2,0:T(8,128)(2,1)S(1)}, u32[]{:S(2)}, u32[]{:S(2)}) collective-permute-start(bf16[1,128,320]{1,2,0:T(8,128)(2,1)S(1)} %get-tuple-element.30), channel_id=1, source_target_pairs={{1,0},{3,2},{5,4},{7,6},{9,8},{11,10},{13,12},{15,14},{17,16},{19,... | collective-permute-start | bytes 245768 | tf_op jit(solution)/shard_map/ppermute | solution.py:15
  176.3 0.9 copy-start.1
  176.3 1.0 copy-start.2
  176.8 1.0 copy-start.6
  176.8 1.0 copy-start.7
  176.8 1.0 copy-start.8
  178.8 132.3 %collective-permute-start.2 = (bf16[1,128,320]{1,2,0:T(8,128)(2,1)S(1)}, bf16[1,128,320]{1,2,0:T(8,128)(2,1)S(1)}, u32[]{:S(2)}, u32[]{:S(2)}) collective-permute-start(bf16[1,128,320]{1,2,0:T(8,128)(2,1)S(1)} %get-tuple-element.25), channel_id=1, source_target_pairs={{0,1},{2,3},{4,5},{6,7},{8,9},{10,11},{12,13},{14,15},{16,17},{18,... | collective-permute-start | bytes 245768 | tf_op jit(solution)/shard_map/ppermute | solution.py:14
  182.2 128.9 %collective-permute-start.3 = (bf16[1,128,320]{1,2,0:T(8,128)(2,1)S(1)}, bf16[1,128,320]{1,2,0:T(8,128)(2,1)S(1)}, u32[]{:S(2)}, u32[]{:S(2)}) collective-permute-start(bf16[1,128,320]{1,2,0:T(8,128)(2,1)S(1)} %get-tuple-element.26), channel_id=1, source_target_pairs={{1,0},{3,2},{5,4},{7,6},{9,8},{11,10},{13,12},{15,14},{17,16},{19,... | collective-permute-start | bytes 245768 | tf_op jit(solution)/shard_map/ppermute | solution.py:15
  312.9 0.7 copy-start.9
Sparse Core Ops, SparseCore 0:
  9.8 136.1 all-gather.2
  147.6 133.4 all-gather.4
where the time goes:
time: 323 us; the launch traced here: 321 us
  waiting for transfers between devices  222 us (69%)
  local copies, waits for them, and re-layouts  68.9 us (21%)
  between operations  13.9 us (4%)
  starting transfers between devices  10.9 us (3%)
    all_gather x2, waiting for transfers between devices, whole_weights(): whole_kernel = lax.all_gather(kernel, 'dp', axis=2, tiled=True)  218 us
    reshape x2, local copies, waits for them, and re-layouts, reorder_whole(): split = whole_kernel.reshape(blocks, 9, channels // blocks, channels)  59.7 us
    ppermute x2, starting transfers between devices, padded_2(): before = lax.ppermute(last, axis, up)  8.29 us
    unnamed x34, local copies, waits for them, and re-layouts  6.57 us
  transfers between devices with their start and end apart: 6, of which 3 were waited for; matrix products, arithmetic and copies ran while one was open for 21% of the time, Pallas kernels for 0%

commit v1 on v0

--- a/solution.py
+++ b/solution.py
@@ -48,7 +48,24 @@
 
 
 def whole_weights(kernel, channels):
-    whole_kernel = lax.all_gather(kernel, "dp", axis=2, tiled=True)
+    item_now = lax.axis_size("dp")
+    r1 = lax.axis_index("dp")
+    block_out, u_next, t_next = (item_now, r1, kernel.shape[2])
+    long_array, all_rows = (kernel, 1)
+    while all_rows < block_out:
+        long_array = jnp.concatenate(
+            [
+                long_array,
+                lax.ppermute(
+                    long_array,
+                    axis_name="dp",
+                    perm=[(idx, (idx - all_rows) % block_out) for idx in range(block_out)],
+                ),
+            ],
+            2,
+        )
+        all_rows = 2 * all_rows
+    whole_kernel = jnp.roll(long_array, u_next * t_next, 2)
     return reorder_whole(whole_kernel, channels)
 
 

time: 323 us -> 162 us (0.50)
  waiting for transfers between devices: 222 us -> 84.4 us
  local copies, waits for them, and re-layouts: 68.9 us -> 37.6 us
  between operations: 13.9 us -> 0.48 us
  other arithmetic: 2.98 us -> 15.1 us
  starting transfers between devices: 10.9 us -> 21 us
    all_gather x2 -> x0, waiting for transfers between devices: 218 us -> none  [whole_weights(): whole_kernel = lax.all_gather(kernel, 'dp', axis=2, tiled=True)]
    ppermute x0 -> x8, waiting for transfers between devices: none -> 83.3 us  [whole_weights(): lax.ppermute(long_array, axis_name='dp', perm=[(idx, (idx - all_rows) % b...]
    reshape x2, local copies, waits for them, and re-layouts: 59.7 us -> 6.97 us  [reorder_whole(): split = whole_kernel.reshape(blocks, 9, channels // blocks, channels)]
    concatenate x0 -> x6, local copies, waits for them, and re-layouts: none -> 19.1 us  [whole_weights(): jnp.concatenate([long_array, lax.ppermute(long_array, axis_name='dp', per...]
    concatenate x0 -> x3, other arithmetic: none -> 11.1 us  [the longest x1 9.07 us: whole_weights(): whole_kernel = jnp.roll(long_array, u_next * t_next, 2)]
    ppermute x0 -> x8, starting transfers between devices: none -> 10.6 us  [whole_weights(): lax.ppermute(long_array, axis_name='dp', perm=[(idx, (idx - all_rows) % b...]
    reshape x12, local copies, waits for them, and re-layouts: 1.06 us -> 5.32 us  [window_at(): return window.reshape(height * columns, depth)]
    unnamed x34 -> x46, local copies, waits for them, and re-layouts: 6.57 us -> 2.5 us
  transfers between devices with their start and end apart: 6 -> 12, of which waited for: 3 -> 7; matrix products, arithmetic and copies ran while one was open for 21% -> 19% of each run, Pallas kernels for 0% -> 0%
where the time goes in v1:
time: 162 us; the launch traced here: 161 us
  waiting for transfers between devices  84.4 us (52%)
  local copies, waits for them, and re-layouts  37.6 us (23%)
  starting transfers between devices  21 us (13%)
  other arithmetic  15.1 us (9%)
  matrix products  2.77 us (2%)
    ppermute x8, waiting for transfers between devices, whole_weights(): lax.ppermute(long_array, axis_name='dp', perm=[(idx, (idx - all_rows) % b...  83.3 us
    concatenate x6, local copies, waits for them, and re-layouts, whole_weights(): jnp.concatenate([long_array, lax.ppermute(long_array, axis_name='dp', per...  19.1 us
    ppermute x8, starting transfers between devices, whole_weights(): lax.ppermute(long_array, axis_name='dp', perm=[(idx, (idx - all_rows) % b...  10.6 us
    concatenate x1, other arithmetic, whole_weights(): whole_kernel = jnp.roll(long_array, u_next * t_next, 2)  9.07 us
    ppermute x2, starting transfers between devices, padded_2(): before = lax.ppermute(last, axis, up)  7.67 us
    reshape x2, local copies, waits for them, and re-layouts, reorder_whole(): split = whole_kernel.reshape(blocks, 9, channels // blocks, channels)  6.97 us
    reshape x12, local copies, waits for them, and re-layouts, window_at(): return window.reshape(height * columns, depth)  5.32 us
  transfers between devices with their start and end apart: 12, of which 7 were waited for; matrix products, arithmetic and copies ran while one was open for 19% of the time, Pallas kernels for 0%

profile of v1, /device:TPU:0, one launch (start us, length us, event | category | flops | bytes accessed | tf_op | source)
XLA Modules:
  0.0 161.3 jit_solution(11446005545301198326)
XLA Ops:
  0.0 5.5 %collective-permute-start.2 = (bf16[4,9,1600]{2,0,1:T(4,128)(2,1)}, bf16[4,9,1600]{2,0,1:T(4,128)(2,1)S(1)}, u32[]{:S(2)}, u32[]{:S(2)}) collective-permute-start(bf16[4,9,1600]{2,0,1:T(4,128)(2,1)} %param.21), channel_id=1, source_target_pairs={{0,30},{2,0},{4,2},{6,4},{8,6},{10,8},{12,10},{14,12},{16,14},{18,... | collective-permute-start | bytes 345608 | tf_op jit(solution)/shard_map/ppermute | solution.py:59
  5.6 0.7 collective-permute-start.8
  6.2 0.7 mul.84
  7.0 0.1 mul.85
  7.1 0.7 sub.44
  7.8 0.1 sub.45
  7.9 1.2 multiply_convert_fusion.3
  9.1 3.4 %collective-permute-start = (bf16[1,128,320]{1,2,0:T(8,128)(2,1)S(1)}, bf16[1,128,320]{1,2,0:T(8,128)(2,1)S(1)}, u32[]{:S(2)}, u32[]{:S(2)}) collective-permute-start(bf16[1,128,320]{1,2,0:T(8,128)(2,1)S(1)} %get-tuple-element.30), channel_id=1, source_target_pairs={{0,1},{2,3},{4,5},{6,7},{8,9},{10,11},{12,13},{14,15},{16,17},{18,... | collective-permute-start | bytes 245768 | tf_op jit(solution)/shard_map/ppermute | solution.py:14
  12.5 1.3 collective-permute-start.1
  13.8 1.1 copy.26
  14.9 1.0 pad_maximum_fusion
  16.0 0.6 collective-permute-start.3
  16.5 1.0 pad_maximum_fusion.1
  17.6 1.5 collective-permute-start.9
  19.1 0.9 multiply_convert_fusion.2
  20.1 0.1 mul.99
  20.2 0.1 sub.51
  20.2 0.1 sub.52
  20.4 4.1 %collective-permute-done.3 = bf16[4,9,3200]{2,0,1:T(4,128)(2,1)S(1)} collective-permute-done((bf16[4,9,3200]{2,0,1:T(4,128)(2,1)S(1)}, bf16[4,9,3200]{2,0,1:T(4,128)(2,1)S(1)}, u32[]{:S(2)}, u32[]{:S(2)}) %collective-permute-start.3) | collective-permute-done | bytes 230432 | tf_op jit(solution)/shard_map/ppermute | solution.py:59
  24.5 1.0 concatenate.73
  25.6 0.5 collective-permute-start.4
  26.1 2.0 %collective-permute-done.9 = bf16[4,9,3200]{2,0,1:T(4,128)(2,1)S(1)} collective-permute-done((bf16[4,9,3200]{2,0,1:T(4,128)(2,1)S(1)}, bf16[4,9,3200]{2,0,1:T(4,128)(2,1)S(1)}, u32[]{:S(2)}, u32[]{:S(2)}) %collective-permute-start.9) | collective-permute-done | bytes 230432 | tf_op jit(solution)/shard_map/ppermute | solution.py:59
  28.1 1.6 concatenate.83
  29.7 0.4 collective-permute-start.10
  30.1 0.3 fusion.7
  30.5 1.0 slice_bitcast_fusion.7
  31.5 7.6 %collective-permute-done.4 = bf16[4,9,6400]{2,0,1:T(4,128)(2,1)S(1)} collective-permute-done((bf16[4,9,6400]{2,0,1:T(4,128)(2,1)S(1)}, bf16[4,9,6400]{2,0,1:T(4,128)(2,1)S(1)}, u32[]{:S(2)}, u32[]{:S(2)}) %collective-permute-start.4) | collective-permute-done | bytes 460832 | tf_op jit(solution)/shard_map/ppermute | solution.py:59
  39.1 1.6 concatenate.74
  40.7 0.1 collective-permute-start.5
  40.7 6.7 %collective-permute-done.10 = bf16[4,9,6400]{2,0,1:T(4,128)(2,1)S(1)} collective-permute-done((bf16[4,9,6400]{2,0,1:T(4,128)(2,1)}, bf16[4,9,6400]{2,0,1:T(4,128)(2,1)S(1)}, u32[]{:S(2)}, u32[]{:S(2)}) %collective-permute-start.10) | collective-permute-done | bytes 460832 | tf_op jit(solution)/shard_map/ppermute | solution.py:59
  47.4 2.9 %concatenate.84 = bf16[4,9,12800]{2,0,1:T(4,128)(2,1)} concatenate(bf16[4,9,1600]{2,0,1:T(4,128)(2,1)S(1)} %copy-done.1, bf16[4,9,1600]{2,0,1:T(4,128)(2,1)S(1)} %collective-permute-done.8, bf16[4,9,3200]{2,0,1:T(4,128)(2,1)S(1)} %collective-permute-done.9, bf16[4,9,6400]{2,0,1:T(4,128)(2,1)S(1)} %collective-permute-done.10), dimensions={2} | concatenate | bytes 1843200 | tf_op jit(solution)/shard_map/concatenate | solution.py:56
  50.2 1.3 collective-permute-start.11
  51.6 1.8 %copy_bitcast_fusion.13 = (bf16[256,320]{0,1:T(8,128)(2,1)}, bf16[256,320]{0,1:T(8,128)(2,1)}) fusion(bf16[2,40,8,128]{3,2,1,0:T(8,128)(2,1)} %get-tuple-element.21, bf16[2,40,8,128]{3,2,1,0:T(8,128)(2,1)} %get-tuple-element.22), kind=kLoop, calls=%fused_computation.88 | loop fusion | bytes 655360 | tf_op jit(solution)/shard_map/reshape | solution.py:41
  53.3 0.8 copy_bitcast_fusion.9
  54.1 1.8 %copy_bitcast_fusion.11 = (bf16[256,320]{0,1:T(8,128)(2,1)}, bf16[256,320]{0,1:T(8,128)(2,1)}) fusion(bf16[2,40,8,128]{3,2,1,0:T(8,128)(2,1)} %get-tuple-element.19, bf16[2,40,8,128]{3,2,1,0:T(8,128)(2,1)} %get-tuple-element.20), kind=kLoop, calls=%fused_computation.86 | loop fusion | bytes 655360 | tf_op jit(solution)/shard_map/reshape | solution.py:41
  55.9 0.8 copy_bitcast_fusion.8
  56.7 49.8 %collective-permute-done.5 = bf16[4,9,12800]{2,0,1:T(4,128)(2,1)} collective-permute-done((bf16[4,9,12800]{2,0,1:T(4,128)(2,1)S(1)}, bf16[4,9,12800]{2,0,1:T(4,128)(2,1)}, u32[]{:S(2)}, u32[]{:S(2)}) %collective-permute-start.5) | collective-permute-done | bytes 921632 | tf_op jit(solution)/shard_map/ppermute | solution.py:59
  106.5 5.4 %concatenate.75 = bf16[4,9,25600]{2,0,1:T(4,128)(2,1)S(1)} concatenate(bf16[4,9,1600]{2,0,1:T(4,128)(2,1)S(1)} %copy-done, bf16[4,9,1600]{2,0,1:T(4,128)(2,1)S(1)} %collective-permute-done.2, bf16[4,9,3200]{2,0,1:T(4,128)(2,1)S(1)} %collective-permute-done.3, bf16[4,9,6400]{2,0,1:T(4,128)(2,1)S(1)} %collective-permute-done.4, bf16[4,9,12800]{2,0,1:T(4,128)(2,1)} %collective-permute-done.5), dimensions={2} | concatenate | bytes 3686400 | tf_op jit(solution)/shard_map/concatenate | solution.py:56
  111.9 13.0 %collective-permute-done.11 = bf16[4,9,12800]{2,0,1:T(4,128)(2,1)} collective-permute-done((bf16[4,9,12800]{2,0,1:T(4,128)(2,1)}, bf16[4,9,12800]{2,0,1:T(4,128)(2,1)}, u32[]{:S(2)}, u32[]{:S(2)}) %collective-permute-start.11) | collective-permute-done | bytes 921632 | tf_op jit(solution)/shard_map/ppermute | solution.py:59
  125.0 6.6 %concatenate.85 = bf16[4,9,25600]{2,0,1:T(4,128)(2,1)} concatenate(bf16[4,9,1600]{2,0,1:T(4,128)(2,1)S(1)} %copy-done.1, bf16[4,9,1600]{2,0,1:T(4,128)(2,1)S(1)} %collective-permute-done.8, bf16[4,9,3200]{2,0,1:T(4,128)(2,1)S(1)} %collective-permute-done.9, bf16[4,9,6400]{2,0,1:T(4,128)(2,1)} %copy-done.2, bf16[4,9,12800]{2,0,1:T(4,128)(2,1)} %collective-permute-done.11), dimensions={2} | concatenate | bytes 3686400 | tf_op jit(solution)/shard_map/concatenate | solution.py:56
  131.5 9.1 %fusion = (bf16[4,9,25600]{2,0,1:T(4,128)(2,1)}, bf16[4,9,25600]{2,0,1:T(4,128)(2,1)}) fusion(s32[]{:T(128)S(6)} %select_n.13, bf16[4,9,25600]{2,0,1:T(4,128)(2,1)} %concatenate.85, bf16[4,9,25600]{2,0,1:T(4,128)(2,1)S(1)} %concatenate.75), kind=kLoop, calls=%fused_computation.6 | loop fusion | flops 7372800 | bytes 7372804 | tf_op jit(solution)/shard_map/jit(_roll_dynamic)/concatenate | solution.py:68
  140.6 3.5 %reshape.125 = bf16[4,9,80,320]{3,2,0,1:T(8,128)(2,1)S(1)} reshape(bf16[4,9,25600]{2,0,1:T(4,128)(2,1)} %get-tuple-element.35) | data formatting | bytes 3686400 | tf_op jit(solution)/shard_map/reshape | solution.py:46
  144.1 0.2 fusion.64
  144.4 0.6 copy-done.7
  145.0 0.1 copy-done.8
  145.1 0.1 copy-done.9
  145.2 0.4 fusion.8
  145.7 0.4 convolution_add_fusion.3
  146.1 0.1 copy-done.5
  146.3 0.6 multiply_convert_fusion
  146.9 0.3 multiply_convert_fusion.1
  147.2 4.3 %collective-permute-start.6 = (bf16[1,128,320]{1,2,0:T(8,128)(2,1)S(1)}, bf16[1,128,320]{1,2,0:T(8,128)(2,1)S(1)}, u32[]{:S(2)}, u32[]{:S(2)}) collective-permute-start(bf16[1,128,320]{1,2,0:T(8,128)(2,1)S(1)} %get-tuple-element.26), channel_id=1, source_target_pairs={{0,1},{2,3},{4,5},{6,7},{8,9},{10,11},{12,13},{14,15},{16,17},{18,... | collective-permute-start | bytes 245768 | tf_op jit(solution)/shard_map/ppermute | solution.py:14
  151.5 1.5 collective-permute-start.7
  153.0 3.5 %reshape.135 = bf16[4,9,80,320]{3,2,0,1:T(8,128)(2,1)S(1)} reshape(bf16[4,9,25600]{2,0,1:T(4,128)(2,1)} %get-tuple-element.34) | data formatting | bytes 3686400 | tf_op jit(solution)/shard_map/reshape | solution.py:46
  156.5 0.2 fusion.63
  156.7 1.1 collective-permute-done.7
  157.9 0.3 select_maximum_fusion
  158.2 0.2 slice_bitcast_fusion.1
  158.7 0.4 fusion.24
  159.2 0.4 convolution_add_fusion.1
  159.6 0.4 convolution_add_fusion
  160.1 0.2 reshape.141
  160.3 0.3 copy-done.3
  160.5 0.8 fusion.52
  (58 shorter events, 0.6 us)
Async XLA Ops:
  0.0 24.5 %copy-start = (bf16[4,9,1600]{2,0,1:T(4,128)(2,1)S(1)}, bf16[4,9,1600]{2,0,1:T(4,128)(2,1)}, u32[]{:S(2)}) copy-start(bf16[4,9,1600]{2,0,1:T(4,128)(2,1)} %param.21) | copy-start | bytes 345604
  0.0 19.0 %copy-start.14 = (f32[320]{0:T(512)S(1)}, f32[320]{0:T(512)}, u32[]{:S(2)}) copy-start(f32[320]{0:T(512)} %param.19) | copy-start | bytes 3844
  0.0 19.0 %copy-start.13 = (f32[320]{0:T(512)S(1)}, f32[320]{0:T(512)}, u32[]{:S(2)}) copy-start(f32[320]{0:T(512)} %param.20) | copy-start | bytes 3844
  0.0 20.0 %copy-start.20 = (f32[1,32]{1,0:T(1,128)S(1)}, f32[1,32]{1,0:T(1,128)}, u32[]{:S(2)}) copy-start(f32[1,32]{1,0:T(1,128)} %param.25) | copy-start | bytes 388
  0.0 20.2 %copy-start.21 = (f32[1,32]{1,0:T(1,128)S(1)}, f32[1,32]{1,0:T(1,128)}, u32[]{:S(2)}) copy-start(f32[1,32]{1,0:T(1,128)} %param.24) | copy-start | bytes 388
  0.0 20.3 %copy-start.19 = (f32[1,320]{1,0:T(1,128)S(1)}, f32[1,320]{1,0:T(1,128)}, u32[]{:S(2)}) copy-start(f32[1,320]{1,0:T(1,128)} %param.23) | copy-start | bytes 3844
  0.0 14.9 %collective-permute-start.2 = (bf16[4,9,1600]{2,0,1:T(4,128)(2,1)}, bf16[4,9,1600]{2,0,1:T(4,128)(2,1)S(1)}, u32[]{:S(2)}, u32[]{:S(2)}) collective-permute-start(bf16[4,9,1600]{2,0,1:T(4,128)(2,1)} %param.21), channel_id=1, source_target_pairs={{0,30},{2,0},{4,2},{6,4},{8,6},{10,8},{12,10},{14,12},{16,14},{18,... | collective-permute-start | bytes 345608 | tf_op jit(solution)/shard_map/ppermute | solution.py:59
  5.6 11.0 %collective-permute-start.8 = (bf16[4,9,1600]{2,0,1:T(4,128)(2,1)}, bf16[4,9,1600]{2,0,1:T(4,128)(2,1)S(1)}, u32[]{:S(2)}, u32[]{:S(2)}) collective-permute-start(bf16[4,9,1600]{2,0,1:T(4,128)(2,1)} %param.28), channel_id=1, source_target_pairs={{0,30},{2,0},{4,2},{6,4},{8,6},{10,8},{12,10},{14,12},{16,14},{18,... | collective-permute-start | bytes 345608 | tf_op jit(solution)/shard_map/ppermute | solution.py:59
  7.0 21.1 %copy-start.1 = (bf16[4,9,1600]{2,0,1:T(4,128)(2,1)S(1)}, bf16[4,9,1600]{2,0,1:T(4,128)(2,1)}, u32[]{:S(2)}) copy-start(bf16[4,9,1600]{2,0,1:T(4,128)(2,1)} %param.28) | copy-start | bytes 345604
  9.1 21.0 %collective-permute-start = (bf16[1,128,320]{1,2,0:T(8,128)(2,1)S(1)}, bf16[1,128,320]{1,2,0:T(8,128)(2,1)S(1)}, u32[]{:S(2)}, u32[]{:S(2)}) collective-permute-start(bf16[1,128,320]{1,2,0:T(8,128)(2,1)S(1)} %get-tuple-element.30), channel_id=1, source_target_pairs={{0,1},{2,3},{4,5},{6,7},{8,9},{10,11},{12,13},{14,15},{16,17},{18,... | collective-permute-start | bytes 245768 | tf_op jit(solution)/shard_map/ppermute | solution.py:14
  12.5 17.6 %collective-permute-start.1 = (bf16[1,128,320]{1,2,0:T(8,128)(2,1)S(1)}, bf16[1,128,320]{1,2,0:T(8,128)(2,1)S(1)}, u32[]{:S(2)}, u32[]{:S(2)}) collective-permute-start(bf16[1,128,320]{1,2,0:T(8,128)(2,1)S(1)} %get-tuple-element.31), channel_id=1, source_target_pairs={{1,0},{3,2},{5,4},{7,6},{9,8},{11,10},{13,12},{15,14},{17,16},{19,... | collective-permute-start | bytes 245768 | tf_op jit(solution)/shard_map/ppermute | solution.py:15
  16.0 8.5 %collective-permute-start.3 = (bf16[4,9,3200]{2,0,1:T(4,128)(2,1)S(1)}, bf16[4,9,3200]{2,0,1:T(4,128)(2,1)S(1)}, u32[]{:S(2)}, u32[]{:S(2)}) collective-permute-start(bf16[4,9,3200]{2,0,1:T(4,128)(2,1)S(1)} %pad_maximum_fusion), channel_id=1, source_target_pairs={{0,28},{2,30},{4,0},{6,2},{8,4},{10,6},{12,8},{14,10},{16,12},{18,... | collective-permute-start | bytes 691208 | tf_op jit(solution)/shard_map/ppermute | solution.py:59
  17.6 10.5 %collective-permute-start.9 = (bf16[4,9,3200]{2,0,1:T(4,128)(2,1)S(1)}, bf16[4,9,3200]{2,0,1:T(4,128)(2,1)S(1)}, u32[]{:S(2)}, u32[]{:S(2)}) collective-permute-start(bf16[4,9,3200]{2,0,1:T(4,128)(2,1)S(1)} %pad_maximum_fusion.1), channel_id=1, source_target_pairs={{0,28},{2,30},{4,0},{6,2},{8,4},{10,6},{12,8},{14,10},{16,12},{18,... | collective-permute-start | bytes 691208 | tf_op jit(solution)/shard_map/ppermute | solution.py:59
  25.6 13.5 %collective-permute-start.4 = (bf16[4,9,6400]{2,0,1:T(4,128)(2,1)S(1)}, bf16[4,9,6400]{2,0,1:T(4,128)(2,1)S(1)}, u32[]{:S(2)}, u32[]{:S(2)}) collective-permute-start(bf16[4,9,6400]{2,0,1:T(4,128)(2,1)S(1)} %concatenate.73), channel_id=1, source_target_pairs={{0,24},{2,26},{4,28},{6,30},{8,0},{10,2},{12,4},{14,6},{16,8},{18,... | collective-permute-start | bytes 1382408 | tf_op jit(solution)/shard_map/ppermute | solution.py:59
  29.7 17.7 %collective-permute-start.10 = (bf16[4,9,6400]{2,0,1:T(4,128)(2,1)}, bf16[4,9,6400]{2,0,1:T(4,128)(2,1)S(1)}, u32[]{:S(2)}, u32[]{:S(2)}) collective-permute-start(bf16[4,9,6400]{2,0,1:T(4,128)(2,1)} %concatenate.83), channel_id=1, source_target_pairs={{0,24},{2,26},{4,28},{6,30},{8,0},{10,2},{12,4},{14,6},{16,8},{18,... | collective-permute-start | bytes 1382408 | tf_op jit(solution)/shard_map/ppermute | solution.py:59
  40.7 65.8 %collective-permute-start.5 = (bf16[4,9,12800]{2,0,1:T(4,128)(2,1)S(1)}, bf16[4,9,12800]{2,0,1:T(4,128)(2,1)}, u32[]{:S(2)}, u32[]{:S(2)}) collective-permute-start(bf16[4,9,12800]{2,0,1:T(4,128)(2,1)S(1)} %concatenate.74), channel_id=1, source_target_pairs={{0,16},{2,18},{4,20},{6,22},{8,24},{10,26},{12,28},{14,30},{16,0},... | collective-permute-start | bytes 2764808 | tf_op jit(solution)/shard_map/ppermute | solution.py:59
  47.4 8.5 %copy-start.2 = (bf16[4,9,6400]{2,0,1:T(4,128)(2,1)}, bf16[4,9,6400]{2,0,1:T(4,128)(2,1)S(1)}, u32[]{:S(2)}) copy-start(bf16[4,9,6400]{2,0,1:T(4,128)(2,1)S(1)} %collective-permute-done.10) | copy-start | bytes 1382404
  50.2 74.7 %collective-permute-start.11 = (bf16[4,9,12800]{2,0,1:T(4,128)(2,1)}, bf16[4,9,12800]{2,0,1:T(4,128)(2,1)}, u32[]{:S(2)}, u32[]{:S(2)}) collective-permute-start(bf16[4,9,12800]{2,0,1:T(4,128)(2,1)} %concatenate.84), channel_id=1, source_target_pairs={{0,16},{2,18},{4,20},{6,22},{8,24},{10,26},{12,28},{14,30},{16,0},... | collective-permute-start | bytes 2764808 | tf_op jit(solution)/shard_map/ppermute | solution.py:59
  144.1 0.9 copy-start.7
  144.1 1.0 copy-start.8
  144.1 1.1 copy-start.9
  144.4 1.3 copy-start.10
  144.4 1.3 copy-start.11
  144.4 1.3 copy-start.12
  145.2 1.0 copy-start.4
  145.2 1.0 copy-start.5
  145.2 1.1 copy-start.6
  145.2 1.1 copy-start.15
  145.2 1.1 copy-start.16
  145.2 1.1 copy-start.17
  147.2 9.5 %collective-permute-start.6 = (bf16[1,128,320]{1,2,0:T(8,128)(2,1)S(1)}, bf16[1,128,320]{1,2,0:T(8,128)(2,1)S(1)}, u32[]{:S(2)}, u32[]{:S(2)}) collective-permute-start(bf16[1,128,320]{1,2,0:T(8,128)(2,1)S(1)} %get-tuple-element.26), channel_id=1, source_target_pairs={{0,1},{2,3},{4,5},{6,7},{8,9},{10,11},{12,13},{14,15},{16,17},{18,... | collective-permute-start | bytes 245768 | tf_op jit(solution)/shard_map/ppermute | solution.py:14
  151.5 6.3 %collective-permute-start.7 = (bf16[1,128,320]{1,2,0:T(8,128)(2,1)S(1)}, bf16[1,128,320]{1,2,0:T(8,128)(2,1)S(1)}, u32[]{:S(2)}, u32[]{:S(2)}) collective-permute-start(bf16[1,128,320]{1,2,0:T(8,128)(2,1)S(1)} %get-tuple-element.27), channel_id=1, source_target_pairs={{1,0},{3,2},{5,4},{7,6},{9,8},{11,10},{13,12},{15,14},{17,16},{19,... | collective-permute-start | bytes 245768 | tf_op jit(solution)/shard_map/ppermute | solution.py:15
  159.6 0.9 copy-start.3
  159.6 0.9 copy-start.18
